TPU v7x, 128 devices: a whole 4x4x4 slice. The times are simulated.
128 devices in a mesh: grp: 2 (over y_lo), tp: 64 (over y_hi, z, x, core).
Axes of the slice: x: 4, y: 4 (y_hi: 2, y_lo: 2; y = y_hi * 2 + y_lo), z: 4, core: 2. Of those that a mesh axis runs over, the one named last changes fastest.
Arguments:
- patches: bfloat16 [5120, 1408], P('tp'), may hold values from -6 to 6
- grids: int32 [64, 3, 2], P('tp'), may hold values from 0 to 40, as said below
- positions: int32 [1280], replicated, may hold values from 0 to 2048, as said below
- vis_gain: float32 [1408], replicated, may hold values from 0.1 to 1.9
- vis_query: bfloat16 [1408, 1408], P(None, 'grp')
- vis_key: bfloat16 [1408, 1408], P(None, 'grp'), may hold values from -0.15625 to 0.15625
- vis_value: bfloat16 [1408, 1408], P(None, 'grp'), may hold values from -0.15625 to 0.15625
- vis_out: bfloat16 [1408, 1408], P('grp'), may hold values from -0.15625 to 0.15625
- w_proj: bfloat16 [5632, 4096], P(None, 'tp'), may hold values from -0.078125 to 0.078125
- text_embed: bfloat16 [2048, 4096], P(('grp', 'tp')), may hold values from -6 to 6
- slots: int32 [2, 512], P('grp'), may hold values from 0 to 1023, as said below
- lengths: int32 [2, 8], P('grp'), may hold values from 1 to 256, 1024 in all within a row
- attn_gain: float32 [4096], replicated, may hold values from 0.1 to 1.9
- mlp_gain: float32 [4096], replicated, may hold values from 0.1 to 1.9
- w_kv: bfloat16 [4096, 8192], P(None, 'tp'), may hold values from -0.09375 to 0.09375
- w_gate: bfloat16 [4096, 11008], P(None, 'tp'), may hold values from -0.09375 to 0.09375
- w_up: bfloat16 [4096, 11008], P(None, 'tp'), may hold values from -0.09375 to 0.09375
- w_down: bfloat16 [11008, 4096], P('tp'), may hold values from -0.0546875 to 0.0546875
Outputs:
- layer_out: bfloat16 [2048, 4096], P(('grp', 'tp'))
- kv_out: bfloat16 [2, 512, 8192], P('grp', None, 'tp')
Inputs may be any that keep to these rules, and one draw needn't show every extreme that they name: `grids`: heights and widths are even; the areas of one tp index sum to at most 80; a height of 0 marks an empty entry. `positions`: every merged cell slot inside an image holds a distinct prompt position below 2048, increasing with the slot; slots past a block's images hold 2048. `slots`: distinct within each batch.
All inputs are finite; a program needn't handle non-finite values.
Results may differ from a plain program's by a relative error of at most 0.014.
The roundings to bfloat16 on the way count: a program that leaves them out, or rounds other values in their place, can miss the bound.
Values may be sent and summed in bfloat16 or wider, within the bound.
A program may use at most 128 MiB of HBM per device.

v0:
```python
import math
import jax
import jax.numpy as jnp
from jax import lax
from jax.sharding import PartitionSpec as P

VHD = 88
HD = 128
PATCH_DEV = 80
MERGE_DEV = 20
IMGS = 3


def layer_norm(row_data, gain_vec):
    as_float = row_data.astype(jnp.float32)
    center = as_float - jnp.mean(as_float, axis=-1, keepdims=True)
    spread = jnp.mean(center * center, axis=-1, keepdims=True)
    return (center * lax.rsqrt(spread + 1e-06) * gain_vec).astype(jnp.bfloat16)


def rms_norm(row_data, gain_vec):
    as_float = row_data.astype(jnp.float32)
    square_mean = jnp.mean(as_float * as_float, axis=-1, keepdims=True)
    return (as_float * lax.rsqrt(square_mean + 1e-05) * gain_vec).astype(jnp.bfloat16)


def image_tables(grid_dev):
    heights = grid_dev[:, 0]
    widths = grid_dev[:, 1]
    areas = heights * widths
    seg_ends = jnp.cumsum(areas)
    slot_ids = jnp.arange(PATCH_DEV, dtype=jnp.int32)
    segment = jnp.sum((slot_ids[:, None] >= seg_ends[None, :]).astype(jnp.int32), axis=1)
    cell_areas = areas // 4
    cell_ends = jnp.cumsum(cell_areas)
    cell_starts = cell_ends - cell_areas
    cell_ids = jnp.arange(MERGE_DEV, dtype=jnp.int32)
    which = jnp.sum((cell_ids[:, None] >= cell_ends[None, :]).astype(jnp.int32), axis=1)
    which = jnp.minimum(which, IMGS - 1)
    select = (which[:, None] == jnp.arange(IMGS, dtype=jnp.int32)[None, :]).astype(jnp.int32)
    start_cell = jnp.sum(select * cell_starts[None, :], axis=1)
    width_sel = jnp.sum(select * widths[None, :], axis=1)
    half_width = jnp.maximum(width_sel // 2, 1)
    inner = cell_ids - start_cell
    row_pair = inner // half_width
    col_pair = inner % half_width
    corner = 4 * start_cell + 2 * row_pair * width_sel + 2 * col_pair
    corners = jnp.stack([corner, corner + 1, corner + width_sel, corner + width_sel + 1], axis=1)
    valid = cell_ids < cell_ends[IMGS - 1]
    return (segment, jnp.where(valid[:, None], corners, 0))


def rotate_keys(values_f, token_pos, first_col):
    col_count = values_f.shape[1]
    col_ids = first_col + jnp.arange(0, col_count, 2, dtype=jnp.int32)
    pair_ids = col_ids % HD // 2
    is_key = col_ids // HD % 2 == 0
    freq = jnp.exp(pair_ids.astype(jnp.float32) * (-2.0 * math.log(10000.0) / HD))
    angle = token_pos.astype(jnp.float32)[:, None] * freq[None, :]
    cosine = jnp.where(is_key[None, :], jnp.cos(angle), 1.0)
    sine = jnp.where(is_key[None, :], jnp.sin(angle), 0.0)
    paired = values_f.reshape(values_f.shape[0], col_count // 2, 2)
    even_part = paired[:, :, 0]
    odd_part = paired[:, :, 1]
    turned = jnp.stack(
        [even_part * cosine - odd_part * sine, even_part * sine + odd_part * cosine], axis=2
    )
    return turned.reshape(values_f.shape[0], col_count)


def slot_positions(slot_ids, length_row):
    req_ends = jnp.cumsum(length_row)
    req_starts = req_ends - length_row
    inside = (slot_ids[:, None] >= req_starts[None, :]) & (slot_ids[:, None] < req_ends[None, :])
    return slot_ids - jnp.sum(jnp.where(inside, req_starts[None, :], 0), axis=1)


def local(
    patches,
    grids,
    positions,
    vis_gain,
    vis_query,
    vis_key,
    vis_value,
    vis_out,
    w_proj,
    text_embed,
    slots,
    lengths,
    attn_gain,
    mlp_gain,
    w_kv,
    w_gate,
    w_up,
    w_down,
):
    segment, corners = image_tables(grids[0])
    normed = layer_norm(patches, vis_gain)
    query_rows = jnp.dot(normed, vis_query, preferred_element_type=jnp.float32).astype(jnp.bfloat16)
    key_rows = jnp.dot(normed, vis_key, preferred_element_type=jnp.float32).astype(jnp.bfloat16)
    value_rows = jnp.dot(normed, vis_value, preferred_element_type=jnp.float32).astype(jnp.bfloat16)
    slot_count = patches.shape[0]
    head_count = query_rows.shape[1] // VHD
    head_query = query_rows.reshape(slot_count, head_count, VHD)
    head_key = key_rows.reshape(slot_count, head_count, VHD)
    head_value = value_rows.reshape(slot_count, head_count, VHD)
    scores = jnp.einsum(
        "qhd,khd->hqk", head_query, head_key, preferred_element_type=jnp.float32
    ) * VHD ** (-0.5)
    allowed = segment[:, None] == segment[None, :]
    scores = jnp.where(allowed[None, :, :], scores, -1e30)
    row_max = jnp.max(scores, axis=-1, keepdims=True)
    expos = jnp.exp(scores - row_max)
    attn_probs = (expos / jnp.sum(expos, axis=-1, keepdims=True)).astype(jnp.bfloat16)
    context = jnp.einsum("hqk,khd->qhd", attn_probs, head_value, preferred_element_type=jnp.float32)
    context = context.reshape(slot_count, head_count * VHD).astype(jnp.bfloat16)
    partial_out = jnp.dot(context, vis_out, preferred_element_type=jnp.float32)
    attended = lax.psum(partial_out.astype(jnp.bfloat16), "grp").astype(jnp.float32)
    vision = (patches.astype(jnp.float32) + attended).astype(jnp.bfloat16)
    merged = vision[corners.reshape(-1)].reshape(corners.shape[0], 4 * patches.shape[1])
    tok_dev = text_embed.shape[0]
    tp_count = lax.axis_size("tp")
    half_tok = tok_dev * tp_count
    group_index = lax.axis_index("grp")
    tp_index = lax.axis_index("tp")
    col_count = w_proj.shape[1]
    image_cols = jnp.dot(
        lax.all_gather(merged, "tp", axis=0, tiled=True), w_proj, preferred_element_type=jnp.float32
    ).astype(jnp.bfloat16)
    local_rows = positions - group_index * half_tok
    inside = (local_rows >= 0) & (local_rows < half_tok)
    local_rows = jnp.where(inside, local_rows, half_tok)
    buffer = (
        jnp.zeros((half_tok, col_count), jnp.bfloat16).at[local_rows].set(image_cols, mode="drop")
    )
    placed = lax.all_to_all(buffer, "tp", split_axis=0, concat_axis=1, tiled=True)
    first_row = (group_index * tp_count + tp_index) * tok_dev
    own_rows = first_row + jnp.arange(tok_dev, dtype=jnp.int32)
    is_image = jnp.any(positions[None, :] == own_rows[:, None], axis=1)
    assembled = jnp.where(is_image[:, None], placed, text_embed)
    token_batch = lax.all_gather(assembled, "tp", axis=0, tiled=True)
    mlp_normed = rms_norm(token_batch, mlp_gain)
    gate_val = jnp.dot(mlp_normed, w_gate, preferred_element_type=jnp.float32)
    up_val = jnp.dot(mlp_normed, w_up, preferred_element_type=jnp.float32)
    hidden = (jax.nn.silu(gate_val) * up_val).astype(jnp.bfloat16)
    every_term = jnp.dot(hidden, w_down, preferred_element_type=jnp.float32)
    every_sum = lax.psum(every_term, "tp")
    mixed = lax.dynamic_slice_in_dim(every_sum, tp_index * tok_dev, tok_dev, 0)
    layer_out = (assembled.astype(jnp.float32) + mixed).astype(jnp.bfloat16)
    slot_ids = slots[0]
    slot_rows = token_batch[slot_ids]
    attn_normed = rms_norm(slot_rows, attn_gain)
    kv_cols = jnp.dot(attn_normed, w_kv, preferred_element_type=jnp.float32)
    token_pos = slot_positions(slot_ids, lengths[0])
    kv_out = rotate_keys(kv_cols, token_pos, tp_index * w_kv.shape[1]).astype(jnp.bfloat16)
    return (layer_out, kv_out[None])


def solution(mesh):
    return jax.shard_map(
        local,
        mesh=mesh,
        in_specs=(
            P("tp", None),
            P("tp", None, None),
            P(),
            P(),
            P(None, "grp"),
            P(None, "grp"),
            P(None, "grp"),
            P("grp", None),
            P(None, "tp"),
            P(("grp", "tp"), None),
            P("grp", None),
            P("grp", None),
            P(),
            P(),
            P(None, "tp"),
            P(None, "tp"),
            P(None, "tp"),
            P("tp", None),
        ),
        out_specs=(P(("grp", "tp"), None), P("grp", None, "tp")),
        check_vma=False,
    )
```

profile of v0, /device:TPU:1, one launch (start us, length us, event | category | flops | bytes accessed | tf_op | source)
XLA Modules:
  0.0 1008.9 jit_solution(15142676936785822267)
XLA Ops:
  7.3 1.2 convert_reduce_fusion
  8.5 1.2 fusion.35
  9.7 0.8 and_select_fusion.8
  10.8 2.4 convolution_convert_fusion.4
  13.5 2.4 convolution_convert_fusion.3
  16.4 2.4 convolution_convert_fusion.5
  19.6 1.2 convolution_convert_fusion
  21.6 0.7 iota_compare_fusion.3
  22.9 30.2 %all-reduce.3.cloned.1.call-done = bf16[80,1408]{1,0:T(8,128)(2,1)} async-done(((bf16[80,1408]{1,0:T(8,128)(2,1)}), bf16[80,1408]{1,0:T(8,128)(2,1)}) %all-reduce.3.cloned.1.call-update) | async-done | bytes 225296 | tf_op jit(solution)/shard_map/psum | solution.py:119
  53.0 1.0 fusion.38
  54.0 0.8 gather_fusion
  54.8 0.9 reshape.653
  55.7 110.1 %all-gather.6.cloned.1.call-done = bf16[64,20,5632]{2,1,0:T(8,128)(2,1)} async-done(((bf16[1,20,5632]{2,1,0:T(8,128)(2,1)}), bf16[64,20,5632]{2,1,0:T(8,128)(2,1)}) %all-gather.6.cloned.1.call-update) | async-done | bytes 14417936 | tf_op jit(solution)/shard_map/all_gather | solution.py:129
  165.9 17.6 %reshape.654 = bf16[1280,5632]{1,0:T(8,128)(2,1)} reshape(bf16[64,20,5632]{2,1,0:T(8,128)(2,1)} %all-gather.6.cloned.1.call-done) | data formatting | bytes 28835840
  183.4 9.6 convolution_convert_fusion.1
  193.2 6.3 scatter_custom_fusion
  199.5 0.8 reshape.658
  200.4 5.9 all-to-all-start
  206.5 9.8 all-to-all-done
  216.9 0.7 broadcast_select_fusion.2
  217.9 77.9 %all-gather.4.cloned.1.call-done = bf16[1024,4096]{1,0:T(8,128)(2,1)} async-done(((bf16[16,4096]{1,0:T(8,128)(2,1)}), bf16[1024,4096]{1,0:T(8,128)(2,1)}) %all-gather.4.cloned.1.call-update) | async-done | bytes 8388624 | tf_op jit(solution)/shard_map/all_gather | solution.py:142
  295.8 5.2 fusion.1
  301.6 4.7 fusion.13
  306.3 11.7 %fusion.22 = f32[1024,4096]{1,0:T(8,128)} fusion(bf16[172,4096]{1,0:T(8,128)(2,1)} %param.35, bf16[4096,172]{0,1:T(8,128)(2,1)S(1)} %copy-done.4, bf16[1024,4096]{1,0:T(8,128)(2,1)} %all-gather.4.cloned.1.call-done, f32[4096]{0:T(1024)S(1)} %copy-done.8, f32[1024]{0:T(1024)S(1)} %add_rsqrt_fusion, f32[1024,172]{0,1:T(8,128)S(1)} %fusion.13), kind=kOutput, calls=%fused_computation.23 | convolution fusion | flops 2903515136 | bytes 28708864 | tf_op jit(solution)/shard_map/dot_general | solution.py:147
  318.1 0.6 copy-done.13
  319.1 13.0 %gather_fusion.1 = bf16[512,4096]{1,0:T(8,128)(2,1)} fusion(bf16[1024,4096]{1,0:T(8,128)(2,1)} %all-gather.4.cloned.1.call-done, s32[1024]{0:T(1024)S(1)} %pad_clamp_fusion), kind=kCustom, calls=%fused_computation.1 | custom fusion | bytes 8390656 | tf_op jit(solution)/shard_map/gather | solution.py:152
  332.1 3.2 fusion.4
  335.4 4.2 fusion.7
  339.7 4.5 subtract_convert_fusion
  344.6 0.8 copy.52
  345.3 655.4 %all-reduce.5.cloned.1.call-done = f32[1024,4096]{1,0:T(8,128)} async-done(((f32[1024,4096]{1,0:T(8,128)}), f32[1024,4096]{1,0:T(8,128)}) %all-reduce.5.cloned.1.call-update) | async-done | bytes 16777232 | tf_op jit(solution)/shard_map/psum | solution.py:148
  1000.7 1.6 add_convert_fusion
  (81 shorter events, 5.9 us)
Async XLA Ops:
  7.2 12.4 %copy-start = (bf16[704,1408]{1,0:T(8,128)(2,1)S(1)}, bf16[704,1408]{1,0:T(8,128)(2,1)}, u32[]{:S(2)}) copy-start(bf16[704,1408]{1,0:T(8,128)(2,1)} %param.25) | copy-start | bytes 5947396
  7.2 45.9 %copy-start.3 = (bf16[80,1408]{1,0:T(8,128)(2,1)S(1)}, bf16[80,1408]{1,0:T(8,128)(2,1)}, u32[]{:S(2)}) copy-start(bf16[80,1408]{1,0:T(8,128)(2,1)} %param.18) | copy-start | bytes 675844
  7.2 14.4 %copy-start.11 = (s32[1,3,2]{1,2,0:T(2,128)S(1)}, s32[1,3,2]{1,2,0:T(2,128)}, u32[]{:S(2)}) copy-start(s32[1,3,2]{1,2,0:T(2,128)} %param.19) | copy-start | bytes 76
  7.2 45.8 %all-reduce.3.cloned.1.call-start = ((), (), s32[]{:S(2)}) async-start(), calls=%async_computation.1 | async-start | bytes 450560 | tf_op jit(solution)/shard_map/psum | solution.py:119
  10.8 44.9 %copy-start.9 = (s32[1280]{0:T(1024)S(1)}, s32[1280]{0:T(1024)}, u32[]{:S(2)}) copy-start(s32[1280]{0:T(1024)} %param.20) | copy-start | bytes 15364
  20.8 145.1 %all-gather.6.cloned.1.call-start = ((), (), s32[]{:S(2)}) async-start(), calls=%async_computation.4 | async-start | bytes 17571840 | tf_op jit(solution)/shard_map/all_gather | solution.py:129
  55.7 127.7 %copy-start.6 = (bf16[5632,64]{0,1:T(8,128)(2,1)S(1)}, bf16[5632,64]{0,1:T(8,128)(2,1)}, u32[]{:S(2)}) copy-start(bf16[5632,64]{0,1:T(8,128)(2,1)} %param.26) | copy-start | bytes 2162692
  183.4 33.5 %copy-start.7 = (bf16[16,4096]{1,0:T(8,128)(2,1)S(1)}, bf16[16,4096]{1,0:T(8,128)(2,1)}, u32[]{:S(2)}) copy-start(bf16[16,4096]{1,0:T(8,128)(2,1)} %param.27) | copy-start | bytes 393220
  193.0 108.1 %copy-start.8 = (f32[4096]{0:T(1024)S(1)}, f32[4096]{0:T(1024)}, u32[]{:S(2)}) copy-start(f32[4096]{0:T(1024)} %param.31) | copy-start | bytes 49156
  200.4 15.9 %all-to-all-start = ((bf16[64,2,512]{2,1,0:T(2,128)(2,1)}), bf16[64,2,512]{2,1,0:T(2,128)(2,1)S(1)}, u32[]{:S(2)}, u32[]{:S(2)}) async-start(bf16[64,2,512]{2,1,0:T(2,128)(2,1)} %reshape.658), calls=%async_computation | async-start | bytes 262144 | tf_op jit(solution)/shard_map/all_to_all | solution.py:137
  206.3 89.5 %all-gather.4.cloned.1.call-start = ((), (), s32[]{:S(2)}) async-start(), calls=%async_computation.2 | async-start | bytes 8519680 | tf_op jit(solution)/shard_map/all_gather | solution.py:142
  217.6 783.1 %all-reduce.5.cloned.1.call-start = ((), (), s32[]{:S(2)}) async-start(), calls=%async_computation.3 | async-start | bytes 33554432 | tf_op jit(solution)/shard_map/psum | solution.py:148
  295.8 5.8 copy-start.2
  301.6 4.7 copy-start.4
  318.0 0.7 copy-start.13
  318.0 0.9 copy-start.10
  319.1 16.3 %copy-start.12 = (f32[4096]{0:T(1024)S(1)}, f32[4096]{0:T(1024)}, u32[]{:S(2)}) copy-start(f32[4096]{0:T(1024)} %param.30) | copy-start | bytes 49156
  332.1 668.6 %copy-start.5 = (bf16[16,4096]{1,0:T(8,128)(2,1)S(1)}, bf16[16,4096]{1,0:T(8,128)(2,1)}, u32[]{:S(2)}) copy-start(bf16[16,4096]{1,0:T(8,128)(2,1)} %broadcast_select_fusion.2) | copy-start | bytes 393220
  332.1 670.3 %copy-start.1 = (bf16[704,1408]{1,0:T(8,128)(2,1)S(1)}, bf16[704,1408]{1,0:T(8,128)(2,1)}, u32[]{:S(2)}) copy-start(bf16[704,1408]{1,0:T(8,128)(2,1)} %param.25) | copy-start | bytes 5947396
Sparse Core Ops, SparseCore 0:
  20.9 32.0 all-reduce.2
  56.3 109.4 all-gather.5
  217.8 77.9 all-gather.3
  318.2 682.4 all-reduce.4
where the time goes:
time: 1010 us
  waiting for transfers between devices  883 us (87%)
  local copies, waits for them, and re-layouts  43.9 us (4%)
  matrix products  39.2 us (4%)
  other arithmetic  21.9 us (2%)
  between operations  14.2 us (1%)
    psum x1, waiting for transfers between devices, local(): every_sum = lax.psum(every_term, 'tp')  655 us
    all_gather x1, waiting for transfers between devices, local(): lax.all_gather(merged, 'tp', axis=0, tiled=True)  110 us
    all_gather x1, waiting for transfers between devices, local(): token_batch = lax.all_gather(assembled, 'tp', axis=0, tiled=True)  77.9 us
    psum x1, waiting for transfers between devices, local(): lax.psum(partial_out.astype(jnp.bfloat16), 'grp').astype(jnp.float32)  30.2 us
    unnamed x33, local copies, waits for them, and re-layouts  21.5 us
  transfers between devices with their start and end apart: 5, of which 5 were waited for; matrix products, arithmetic and copies ran while one was open for 3% of the time, Pallas kernels for 0%

commit v1 on v0

--- a/solution.py
+++ b/solution.py
@@ -126,7 +126,11 @@
     tp_index = lax.axis_index("tp")
     col_count = w_proj.shape[1]
     image_cols = jnp.dot(
-        lax.all_gather(merged, "tp", axis=0, tiled=True), w_proj, preferred_element_type=jnp.float32
+        jnp.concatenate(
+            lax.all_to_all(jnp.stack([merged] * lax.axis_size("tp")), "tp", 0, 0), axis=0
+        ),
+        w_proj,
+        preferred_element_type=jnp.float32,
     ).astype(jnp.bfloat16)
     local_rows = positions - group_index * half_tok
     inside = (local_rows >= 0) & (local_rows < half_tok)

time: 1010 us -> 1170 us (1.16)
  waiting for transfers between devices: 883 us -> 1020 us
  starting transfers between devices: 6.23 us -> 30.1 us
    all_to_all x0 -> x1, waiting for transfers between devices: none -> 245 us  [local(): lax.all_to_all(jnp.stack([merged] * lax.axis_size('tp')), 'tp', 0, 0)]
    all_gather x1 -> x0, waiting for transfers between devices: 110 us -> none  [local(): lax.all_gather(merged, 'tp', axis=0, tiled=True)]
    unnamed x33 -> x31, local copies, waits for them, and re-layouts: 21.5 us -> 3.03 us
    reshape x0 -> x1, local copies, waits for them, and re-layouts: none -> 17.6 us  [local(): jnp.concatenate(lax.all_to_all(jnp.stack([merged] * lax.axis_size('tp')),...]
    all_to_all x1, starting transfers between devices: 5.88 us -> 18.8 us  [local(): lax.all_to_all(buffer, 'tp', split_axis=0, concat_axis=1, tiled=True)]
  transfers between devices with their start and end apart: 5 -> 5, of which waited for: 5 -> 5; matrix products, arithmetic and copies ran while one was open for 3% -> 2% of each run, Pallas kernels for 0% -> 0%
where the time goes in v1:
time: 1170 us
  waiting for transfers between devices  1020 us (87%)
  local copies, waits for them, and re-layouts  49.4 us (4%)
  matrix products  39.2 us (3%)
  starting transfers between devices  30.1 us (3%)
  other arithmetic  21.9 us (2%)
  between operations  14.2 us (1%)
    psum x1, waiting for transfers between devices, local(): every_sum = lax.psum(every_term, 'tp')  655 us
    all_to_all x1, waiting for transfers between devices, local(): lax.all_to_all(jnp.stack([merged] * lax.axis_size('tp')), 'tp', 0, 0)  245 us
    all_gather x1, waiting for transfers between devices, local(): token_batch = lax.all_gather(assembled, 'tp', axis=0, tiled=True)  77.1 us
    psum x1, waiting for transfers between devices, local(): lax.psum(partial_out.astype(jnp.bfloat16), 'grp').astype(jnp.float32)  30.2 us
  transfers between devices with their start and end apart: 5, of which 5 were waited for; matrix products, arithmetic and copies ran while one was open for 2% of the time, Pallas kernels for 0%

profile of v1, /device:TPU:1, one launch (start us, length us, event | category | flops | bytes accessed | tf_op | source)
XLA Modules:
  0.0 1171.6 jit_solution(6493756852267856910)
XLA Ops:
  7.2 0.8 and_select_fusion.8
  8.1 1.1 convert_reduce_fusion
  9.2 1.2 fusion.35
  10.4 2.4 convolution_convert_fusion.4
  13.0 2.4 convolution_convert_fusion.3
  16.4 2.4 convolution_convert_fusion.5
  19.5 1.2 convolution_convert_fusion
  21.8 0.7 iota_compare_fusion.3
  22.7 30.2 %all-reduce.3.cloned.1.call-done = bf16[80,1408]{1,0:T(8,128)(2,1)} async-done(((bf16[80,1408]{1,0:T(8,128)(2,1)}), bf16[80,1408]{1,0:T(8,128)(2,1)}) %all-reduce.3.cloned.1.call-update) | async-done | bytes 225296 | tf_op jit(solution)/shard_map/psum | solution.py:119
  53.0 1.0 fusion.38
  54.0 0.8 gather_fusion
  54.9 6.2 stack.8
  61.1 10.9 all-to-all-start
  72.1 244.5 %all-to-all-done = bf16[64,20,5632]{2,1,0:T(8,128)(2,1)} async-done(((bf16[64,20,5632]{2,1,0:T(8,128)(2,1)}), bf16[64,20,5632]{2,1,0:T(8,128)(2,1)}, u32[]{:S(2)}, u32[]{:S(2)}) %all-to-all-start) | async-done | bytes 14417952 | tf_op jit(solution)/shard_map/all_to_all | solution.py:130
  316.6 17.6 %reshape.626 = bf16[1280,5632]{1,0:T(8,128)(2,1)} reshape(bf16[64,20,5632]{2,1,0:T(8,128)(2,1)} %all-to-all-done) | data formatting | bytes 28835840 | tf_op jit(solution)/shard_map/reshape | solution.py:129
  334.2 9.6 convolution_convert_fusion.1
  344.0 6.3 scatter_custom_fusion
  350.3 0.8 reshape.657
  351.1 18.8 %all-to-all-start.1 = ((bf16[64,2,512]{2,1,0:T(2,128)(2,1)}), bf16[64,2,512]{2,1,0:T(2,128)(2,1)S(1)}, u32[]{:S(2)}, u32[]{:S(2)}) async-start(bf16[64,2,512]{2,1,0:T(2,128)(2,1)} %reshape.657), calls=%async_computation.1 | async-start | bytes 262144 | tf_op jit(solution)/shard_map/all_to_all | solution.py:141
  370.2 9.8 all-to-all-done.1
  380.6 0.7 broadcast_select_fusion.2
  381.6 77.1 %all-gather.2.cloned.1.call-done = bf16[1024,4096]{1,0:T(8,128)(2,1)} async-done(((bf16[16,4096]{1,0:T(8,128)(2,1)}), bf16[1024,4096]{1,0:T(8,128)(2,1)}) %all-gather.2.cloned.1.call-update) | async-done | bytes 8388624 | tf_op jit(solution)/shard_map/all_gather | solution.py:146
  458.7 5.2 fusion.1
  464.5 4.7 fusion.13
  469.2 11.7 %fusion.22 = f32[1024,4096]{1,0:T(8,128)} fusion(bf16[172,4096]{1,0:T(8,128)(2,1)} %param.35, bf16[4096,172]{0,1:T(8,128)(2,1)S(1)} %copy-done.4, bf16[1024,4096]{1,0:T(8,128)(2,1)} %all-gather.2.cloned.1.call-done, f32[4096]{0:T(1024)S(1)} %copy-done.8, f32[1024]{0:T(1024)S(1)} %add_rsqrt_fusion, f32[1024,172]{0,1:T(8,128)S(1)} %fusion.13), kind=kOutput, calls=%fused_computation.23 | convolution fusion | flops 2903515136 | bytes 28708864 | tf_op jit(solution)/shard_map/dot_general | solution.py:151
  482.0 13.0 %gather_fusion.1 = bf16[512,4096]{1,0:T(8,128)(2,1)} fusion(bf16[1024,4096]{1,0:T(8,128)(2,1)} %all-gather.2.cloned.1.call-done, s32[1024]{0:T(1024)S(1)} %pad_clamp_fusion), kind=kCustom, calls=%fused_computation.1 | custom fusion | bytes 8390656 | tf_op jit(solution)/shard_map/gather | solution.py:156
  495.0 3.2 fusion.4
  498.2 4.2 fusion.7
  502.6 4.5 subtract_convert_fusion
  507.4 0.8 copy.43
  508.2 655.2 %all-reduce.5.cloned.1.call-done = f32[1024,4096]{1,0:T(8,128)} async-done(((f32[1024,4096]{1,0:T(8,128)}), f32[1024,4096]{1,0:T(8,128)}) %all-reduce.5.cloned.1.call-update) | async-done | bytes 16777232 | tf_op jit(solution)/shard_map/psum | solution.py:152
  1163.4 1.6 add_convert_fusion
  (81 shorter events, 6.6 us)
Async XLA Ops:
  7.2 12.4 %copy-start = (bf16[704,1408]{1,0:T(8,128)(2,1)S(1)}, bf16[704,1408]{1,0:T(8,128)(2,1)}, u32[]{:S(2)}) copy-start(bf16[704,1408]{1,0:T(8,128)(2,1)} %param.25) | copy-start | bytes 5947396
  7.2 13.7 %copy-start.11 = (s32[1,3,2]{1,2,0:T(2,128)S(1)}, s32[1,3,2]{1,2,0:T(2,128)}, u32[]{:S(2)}) copy-start(s32[1,3,2]{1,2,0:T(2,128)} %param.19) | copy-start | bytes 76
  7.2 45.8 %copy-start.3 = (bf16[80,1408]{1,0:T(8,128)(2,1)S(1)}, bf16[80,1408]{1,0:T(8,128)(2,1)}, u32[]{:S(2)}) copy-start(bf16[80,1408]{1,0:T(8,128)(2,1)} %param.18) | copy-start | bytes 675844
  7.2 45.8 %all-reduce.3.cloned.1.call-start = ((), (), s32[]{:S(2)}) async-start(), calls=%async_computation.2 | async-start | bytes 450560 | tf_op jit(solution)/shard_map/psum | solution.py:119
  61.1 11.0 copy-start.9
  61.1 255.5 %all-to-all-start = ((bf16[64,20,5632]{2,1,0:T(8,128)(2,1)}), bf16[64,20,5632]{2,1,0:T(8,128)(2,1)}, u32[]{:S(2)}, u32[]{:S(2)}) async-start(bf16[64,20,5632]{2,1,0:T(8,128)(2,1)} %stack.8), calls=%async_computation | async-start | bytes 34603008 | tf_op jit(solution)/shard_map/all_to_all | solution.py:130
  72.1 262.1 %copy-start.6 = (bf16[5632,64]{0,1:T(8,128)(2,1)S(1)}, bf16[5632,64]{0,1:T(8,128)(2,1)}, u32[]{:S(2)}) copy-start(bf16[5632,64]{0,1:T(8,128)(2,1)} %param.26) | copy-start | bytes 2162692
  334.2 46.4 %copy-start.7 = (bf16[16,4096]{1,0:T(8,128)(2,1)S(1)}, bf16[16,4096]{1,0:T(8,128)(2,1)}, u32[]{:S(2)}) copy-start(bf16[16,4096]{1,0:T(8,128)(2,1)} %param.27) | copy-start | bytes 393220
  343.8 120.2 %copy-start.8 = (f32[4096]{0:T(1024)S(1)}, f32[4096]{0:T(1024)}, u32[]{:S(2)}) copy-start(f32[4096]{0:T(1024)} %param.31) | copy-start | bytes 49156
  351.1 28.9 %all-to-all-start.1 = ((bf16[64,2,512]{2,1,0:T(2,128)(2,1)}), bf16[64,2,512]{2,1,0:T(2,128)(2,1)S(1)}, u32[]{:S(2)}, u32[]{:S(2)}) async-start(bf16[64,2,512]{2,1,0:T(2,128)(2,1)} %reshape.657), calls=%async_computation.1 | async-start | bytes 262144 | tf_op jit(solution)/shard_map/all_to_all | solution.py:141
  370.0 88.7 %all-gather.2.cloned.1.call-start = ((), (), s32[]{:S(2)}) async-start(), calls=%async_computation.3 | async-start | bytes 8519680 | tf_op jit(solution)/shard_map/all_gather | solution.py:146
  381.4 782.0 %all-reduce.5.cloned.1.call-start = ((), (), s32[]{:S(2)}) async-start(), calls=%async_computation.4 | async-start | bytes 33554432 | tf_op jit(solution)/shard_map/psum | solution.py:152
  458.7 5.8 copy-start.2
  464.5 4.7 copy-start.4
  480.9 0.7 copy-start.13
  480.9 0.9 copy-start.10
  482.0 16.3 %copy-start.12 = (f32[4096]{0:T(1024)S(1)}, f32[4096]{0:T(1024)}, u32[]{:S(2)}) copy-start(f32[4096]{0:T(1024)} %param.30) | copy-start | bytes 49156
  495.0 668.4 %copy-start.5 = (bf16[16,4096]{1,0:T(8,128)(2,1)S(1)}, bf16[16,4096]{1,0:T(8,128)(2,1)}, u32[]{:S(2)}) copy-start(bf16[16,4096]{1,0:T(8,128)(2,1)} %broadcast_select_fusion.2) | copy-start | bytes 393220
  495.0 670.1 %copy-start.1 = (bf16[704,1408]{1,0:T(8,128)(2,1)S(1)}, bf16[704,1408]{1,0:T(8,128)(2,1)}, u32[]{:S(2)}) copy-start(bf16[704,1408]{1,0:T(8,128)(2,1)} %param.25) | copy-start | bytes 5947396
Sparse Core Ops, SparseCore 0:
  20.8 32.0 all-reduce.2
  381.5 77.1 all-gather.1
  481.1 682.2 all-reduce.4
